TPU v7x, 512 devices: a whole 4x4x16 slice. The times are simulated.
512 devices in a mesh: region: 16 (over z), slab: 32 (over x, y, core).
Axes of the slice: x: 4, y: 4, z: 16, core: 2. Of those that a mesh axis runs over, the one named last changes fastest.
Arguments:
- records: bfloat16 [16384, 4096], P('region', 'slab'), may hold values from -6 to 6
- first_station: int32 [65536], P(('region', 'slab')), may hold values from 0 to 1023
- second_region: int32 [65536, 1], P(('region', 'slab')), may hold values from 0 to 15; in each aligned block of 128 rows (0 to 127, 128 to 255, ...) at most 16 rows name the same one
- second_station: int32 [65536], P(('region', 'slab')), may hold values from 0 to 1023
Outputs:
- stacks: bfloat16 [65536, 2048], P(('region', 'slab'))
Inputs may be any that keep to these rules, and one draw needn't show every extreme that they name: `second_region`: no region is named by more than 16 pairs of one device.
All inputs are finite; a program needn't handle non-finite values.
Results may differ from a plain program's by a relative error of at most 0.0077.
Values may be sent and summed in bfloat16 or wider, within the bound.
A program may use at most 64 MiB of HBM per device.

v0:
```python
import math
import jax
import jax.numpy as jnp
from jax import lax
from jax.sharding import PartitionSpec as P

NFFT = 2048
BINS = 1024
SEG = 2
HALF = 4


def dft_table():
    sample = jnp.arange(NFFT, dtype=jnp.int32)[:, None]
    frequency = jnp.arange(BINS, dtype=jnp.int32)[None, :]
    phase = (sample * frequency % NFFT).astype(jnp.float32) * (2.0 * math.pi / NFFT)
    return jnp.concatenate([jnp.cos(phase), -jnp.sin(phase)], axis=1).astype(jnp.bfloat16)


def whitened(traces):
    count = traces.shape[0]
    signal = traces.astype(jnp.float32).reshape(count * SEG, NFFT)
    signal = signal - jnp.mean(signal, axis=1, keepdims=True)
    position = jnp.arange(NFFT, dtype=jnp.int32).astype(jnp.float32)
    taper = 0.5 - 0.5 * jnp.cos(position * (2.0 * math.pi / NFFT))
    tapered = (signal * taper[None, :]).astype(jnp.bfloat16)
    spectrum = jnp.dot(tapered, dft_table(), preferred_element_type=jnp.float32)
    real_part = spectrum[:, :BINS]
    imag_part = spectrum[:, BINS:]
    amplitude = jnp.sqrt(real_part * real_part + imag_part * imag_part + 1e-06)
    padded = jnp.pad(amplitude, ((0, 0), (HALF, HALF)))
    smooth = jnp.zeros_like(amplitude)
    for offset in range(2 * HALF + 1):
        smooth = smooth + padded[:, offset : offset + BINS]
    smooth = smooth / (2 * HALF + 1)
    level = jnp.mean(amplitude, axis=1, keepdims=True)
    divisor = smooth + level + 1e-06
    white = spectrum / jnp.concatenate([divisor, divisor], axis=1)
    return white.astype(jnp.bfloat16).reshape(count, SEG * NFFT)


def cross(first_rows, second_rows):
    left = first_rows.astype(jnp.float32).reshape(first_rows.shape[:-1] + (SEG, 2, BINS))
    right = second_rows.astype(jnp.float32).reshape(second_rows.shape[:-1] + (SEG, 2, BINS))
    real_sum = jnp.mean(
        left[..., 0, :] * right[..., 0, :] + left[..., 1, :] * right[..., 1, :], axis=-2
    )
    imag_sum = jnp.mean(
        left[..., 0, :] * right[..., 1, :] - left[..., 1, :] * right[..., 0, :], axis=-2
    )
    return jnp.concatenate([real_sum, imag_sum], axis=-1).astype(jnp.bfloat16)


def local(records, first_station, second_region, second_station):
    regions = lax.axis_size("region")
    pair_count = first_station.shape[0]
    capacity = max(2, pair_count // regions + pair_count // 16)
    arrived = lax.all_to_all(records, "slab", split_axis=0, concat_axis=1, tiled=True)
    spectra = whitened(arrived)
    width = spectra.shape[1]
    target = second_region[:, 0]
    onehot = (target[:, None] == jnp.arange(regions, dtype=jnp.int32)[None, :]).astype(jnp.int32)
    ranking = jnp.sum((jnp.cumsum(onehot, axis=0) - onehot) * onehot, axis=1)
    slot_index = target * capacity + ranking
    requests = (
        jnp.zeros((regions * capacity,), jnp.int32)
        .at[slot_index]
        .set(second_station)
        .reshape(regions, capacity)
    )
    incoming = lax.all_to_all(requests, "region", split_axis=0, concat_axis=0, tiled=True)
    wanted = jnp.concatenate([first_station, incoming.reshape(-1)])
    initial = jnp.zeros((wanted.shape[0], width), jnp.bfloat16)
    piece = lax.all_gather(spectra, "slab", axis=0, tiled=True)
    inside = (wanted >= 0) & (wanted < piece.shape[0])
    chosen = jnp.take(piece, jnp.clip(wanted, 0, piece.shape[0] - 1), axis=0)
    picked = jnp.where(inside[:, None], chosen, initial)
    first_rows = picked[:pair_count]
    served = picked[pair_count:]
    returned = lax.all_to_all(
        served.reshape(regions, capacity, width), "region", split_axis=0, concat_axis=0, tiled=True
    )
    second_rows = jnp.take(returned.reshape(regions * capacity, width), slot_index, axis=0)
    stacks = cross(first_rows, second_rows)
    return stacks


def solution(mesh):
    placed = (
        P("region", "slab"),
        P(("region", "slab")),
        P(("region", "slab"), None),
        P(("region", "slab")),
    )
    return jax.shard_map(
        local, mesh=mesh, in_specs=placed, out_specs=P(("region", "slab"), None), check_vma=False
    )
```

profile of v0, /device:TPU:32, one launch (start us, length us, event | category | flops | bytes accessed | tf_op | source)
XLA Modules:
  0.0 269.8 jit_solution(3383094113395302440)
XLA Ops:
  6.5 7.3 %all-to-all-start.1 = ((bf16[32,32,128]{2,1,0:T(8,128)(2,1)}), bf16[32,32,128]{2,1,0:T(8,128)(2,1)S(1)}, u32[]{:S(2)}, u32[]{:S(2)}) async-start(bf16[32,32,128]{2,1,0:T(8,128)(2,1)} %bitcast.20), calls=%async_computation.1 | async-start | bytes 524288 | tf_op jit(solution)/shard_map/all_to_all | solution.py:58
  13.9 0.0 all-gather.2.cloned.1.call-start
  13.9 34.9 %negate_convert_fusion = (bf16[2048,1024]{1,0:T(8,128)(2,1)}, bf16[2048,1024]{1,0:T(8,128)(2,1)}) fusion(), kind=kLoop, calls=%fused_computation.13 | loop fusion | flops 35651584 | bytes 8388608 | tf_op jit(solution)/shard_map/convert.6
  48.9 0.1 multiply_subtract_fusion
  48.9 0.0 all-to-all-done.1
  48.9 0.2 convert_reduce_fusion
  49.1 0.1 copy.8
  49.2 0.1 reduce_sum.60
  49.3 0.1 reduce_sum.61
  49.4 0.1 convert_bitcast_fusion
  49.5 0.3 copy.7
  49.8 0.1 reshape.149
  49.9 0.0 copy-start.2
  49.9 0.0 copy-start.3
  49.9 4.4 %fusion.3 = f32[64,2048]{1,0:T(8,128)S(1)} fusion(bf16[2048,1024]{1,0:T(8,128)(2,1)} %get-tuple-element.13, bf16[2048,1024]{1,0:T(8,128)(2,1)} %get-tuple-element.14, f32[64,2048]{1,0:T(8,128)S(1)} %reshape.149, f32[2048]{0:T(1024)S(1)} %multiply_subtract_fusion, f32[64]{0:T(128)S(1)} %broadcast_multiply_fusion.1), kind=kOutput, calls=%fused_computation.9 | convolution fusion | flops 554041344 | bytes 9445632 | tf_op jit(solution)/shard_map/dot_general | solution.py:27
  54.3 0.2 fusion.33
  54.5 0.6 fusion.22
  55.2 0.1 fusion.11
  55.2 0.8 reshape.144
  56.0 0.0 all-gather.2.cloned.1.call-update
  56.0 0.0 copy-done.2
  56.0 0.1 fusion.28
  56.1 0.2 reduce_window_sum.11
  56.3 0.2 select_reduce_fusion
  56.5 1.1 scatter_custom_fusion
  57.6 0.7 all_to_all.19
  58.3 15.2 %all-to-all-start = ((s32[16,1,16]{2,1,0:T(1,128)}), s32[16,1,16]{2,1,0:T(1,128)S(1)}, u32[]{:S(2)}, u32[]{:S(2)}) async-start(s32[16,1,16]{2,1,0:T(1,128)} %all_to_all.19), calls=%async_computation | async-start | bytes 16384 | tf_op jit(solution)/shard_map/all_to_all | solution.py:71
  73.5 0.0 copy-done.3
  73.5 11.0 %all-to-all-done = s32[16,1,16]{2,1,0:T(1,128)S(1)} async-done(((s32[16,1,16]{2,1,0:T(1,128)}), s32[16,1,16]{2,1,0:T(1,128)S(1)}, u32[]{:S(2)}, u32[]{:S(2)}) %all-to-all-start) | async-done | bytes 1056 | tf_op jit(solution)/shard_map/all_to_all | solution.py:71
  84.6 0.1 concatenate.43
  84.6 0.5 broadcast.142
  85.1 0.6 reduce.12
  85.7 0.1 concatenate.38
  85.9 42.7 %all-gather.2.cloned.1.call-done = bf16[1024,4096]{1,0:T(8,128)(2,1)} async-done(((bf16[32,4096]{1,0:T(8,128)(2,1)}), bf16[1024,4096]{1,0:T(8,128)(2,1)}) %all-gather.2.cloned.1.call-update) | async-done | bytes 8388624 | tf_op jit(solution)/shard_map/all_gather | solution.py:74
  128.6 12.0 %gather_fusion = bf16[384,4096]{1,0:T(8,128)(2,1)S(1)} fusion(bf16[1024,4096]{1,0:T(8,128)(2,1)} %all-gather.2.cloned.1.call-done, s32[1024]{0:T(1024)S(1)} %pad_clamp_fusion.1), kind=kCustom, calls=%fused_computation | custom fusion | bytes 6292992 | tf_op jit(solution)/shard_map/jit(_take)/gather | solution.py:76
  140.5 0.5 select_select_fusion
  141.0 0.0 copy-start
  141.0 1.7 copy-done
  142.7 1.5 slice.77
  144.2 12.7 %all-to-all-start.2 = ((bf16[16,16,4096]{2,1,0:T(8,128)(2,1)}), bf16[16,16,4096]{2,1,0:T(8,128)(2,1)S(1)}, u32[]{:S(2)}, u32[]{:S(2)}) async-start(bf16[16,16,4096]{2,1,0:T(8,128)(2,1)} %bitcast.19), calls=%async_computation.2 | async-start | bytes 4194304 | tf_op jit(solution)/shard_map/all_to_all | solution.py:80
  156.9 2.8 %slice_convert_fusion = f32[128,4096]{1,0:T(8,128)} fusion(bf16[384,4096]{1,0:T(8,128)(2,1)} %copy-done), kind=kLoop, calls=%fused_computation.21 | loop fusion | flops 524288 | bytes 3145728 | tf_op jit(solution)/shard_map/reshape | solution.py:43
  159.7 4.0 %reshape.151 = f32[128,2,2,1024]{3,2,1,0:T(2,128)} reshape(f32[128,4096]{1,0:T(8,128)} %slice_convert_fusion) | data formatting | bytes 4194304 | tf_op jit(solution)/shard_map/reshape | solution.py:43
  163.7 87.5 %all-to-all-done.2 = bf16[16,16,4096]{2,1,0:T(8,128)(2,1)S(1)} async-done(((bf16[16,16,4096]{2,1,0:T(8,128)(2,1)}), bf16[16,16,4096]{2,1,0:T(8,128)(2,1)S(1)}, u32[]{:S(2)}, u32[]{:S(2)}) %all-to-all-start.2) | async-done | bytes 2097184 | tf_op jit(solution)/shard_map/all_to_all | solution.py:80
  251.2 1.2 gather_fusion.1
  252.4 0.0 copy-start.1
  252.4 1.6 gather.12
  254.0 2.2 fusion.10
  256.2 0.0 copy-done.1
  256.2 5.8 %add_reduce_fusion = (f32[128,1024]{1,0:T(8,128)S(1)}, f32[128,1024]{1,0:T(8,128)S(1)}) fusion(f32[128,2,2,1024]{3,2,1,0:T(2,128)S(1)} %fusion.10, f32[128,2,2,1024]{3,2,1,0:T(2,128)S(1)} %copy-done.1), kind=kLoop, calls=%fused_computation.23 | loop fusion | flops 1835008 | bytes 5242880 | tf_op jit(solution)/shard_map/reduce_sum | solution.py:45
  262.1 0.8 pad_maximum_fusion
  (12 shorter events, 0.2 us)
Async XLA Ops:
  6.5 42.4 %all-to-all-start.1 = ((bf16[32,32,128]{2,1,0:T(8,128)(2,1)}), bf16[32,32,128]{2,1,0:T(8,128)(2,1)S(1)}, u32[]{:S(2)}, u32[]{:S(2)}) async-start(bf16[32,32,128]{2,1,0:T(8,128)(2,1)} %bitcast.20), calls=%async_computation.1 | async-start | bytes 524288 | tf_op jit(solution)/shard_map/all_to_all | solution.py:58
  13.9 114.7 %all-gather.2.cloned.1.call-start = ((), (), s32[]{:S(2)}) async-start(), calls=%async_computation.3 | async-start | bytes 8650752 | tf_op jit(solution)/shard_map/all_gather | solution.py:74
  49.9 6.2 %copy-start.2 = (s32[128,1]{0,1:T(1,128)S(1)}, s32[128,1]{0,1:T(1,128)}, u32[]{:S(2)}) copy-start(s32[128,1]{0,1:T(1,128)} %param.6) | copy-start | bytes 1540
  49.9 23.6 %copy-start.3 = (s32[128]{0:T(128)S(1)}, s32[128]{0:T(128)}, u32[]{:S(2)}) copy-start(s32[128]{0:T(128)} %param.5) | copy-start | bytes 1540
  58.3 26.3 %all-to-all-start = ((s32[16,1,16]{2,1,0:T(1,128)}), s32[16,1,16]{2,1,0:T(1,128)S(1)}, u32[]{:S(2)}, u32[]{:S(2)}) async-start(s32[16,1,16]{2,1,0:T(1,128)} %all_to_all.19), calls=%async_computation | async-start | bytes 16384 | tf_op jit(solution)/shard_map/all_to_all | solution.py:71
  141.0 1.7 copy-start
  144.2 107.0 %all-to-all-start.2 = ((bf16[16,16,4096]{2,1,0:T(8,128)(2,1)}), bf16[16,16,4096]{2,1,0:T(8,128)(2,1)S(1)}, u32[]{:S(2)}, u32[]{:S(2)}) async-start(bf16[16,16,4096]{2,1,0:T(8,128)(2,1)} %bitcast.19), calls=%async_computation.2 | async-start | bytes 4194304 | tf_op jit(solution)/shard_map/all_to_all | solution.py:80
  252.4 3.8 %copy-start.1 = (f32[128,2,2,1024]{3,2,1,0:T(2,128)S(1)}, f32[128,2,2,1024]{3,2,1,0:T(2,128)}, u32[]{:S(2)}) copy-start(f32[128,2,2,1024]{3,2,1,0:T(2,128)} %reshape.151) | copy-start | bytes 6291460
Sparse Core Ops, SparseCore 0:
  56.2 72.3 all-gather.1
where the time goes:
time: 270 us
  waiting for transfers between devices  141 us (52%)
  other arithmetic  49.5 us (18%)
  starting transfers between devices  35.2 us (13%)
  local copies, waits for them, and re-layouts  25.8 us (10%)
  between operations  13.6 us (5%)
  matrix products  4.41 us (2%)
    all_to_all x1, waiting for transfers between devices, local(): lax.all_to_all(served.reshape(regions, capacity, width), 'region', split_...  87.5 us
    all_gather x1, waiting for transfers between devices, local(): piece = lax.all_gather(spectra, 'slab', axis=0, tiled=True)  42.7 us
    another operation x3, other arithmetic  35 us
    all_to_all x1, starting transfers between devices, local(): lax.all_to_all(requests, 'region', split_axis=0, concat_axis=0, tiled=True)  15.2 us
    all_to_all x1, starting transfers between devices, local(): lax.all_to_all(served.reshape(regions, capacity, width), 'region', split_...  12.7 us
    gather x1, local copies, waits for them, and re-layouts, local(): chosen = jnp.take(piece, jnp.clip(wanted, 0, piece.shape[0] - 1), axis=0)  12 us
    all_to_all x1, waiting for transfers between devices, local(): lax.all_to_all(requests, 'region', split_axis=0, concat_axis=0, tiled=True)  11 us
    all_to_all x1, starting transfers between devices, local(): lax.all_to_all(records, 'slab', split_axis=0, concat_axis=1, tiled=True)  7.32 us
  transfers between devices with their start and end apart: 4, of which 3 were waited for; matrix products, arithmetic and copies ran while one was open for 17% of the time, Pallas kernels for 0%

commit v1 on v0

--- a/solution.py
+++ b/solution.py
@@ -71,7 +71,15 @@
     incoming = lax.all_to_all(requests, "region", split_axis=0, concat_axis=0, tiled=True)
     wanted = jnp.concatenate([first_station, incoming.reshape(-1)])
     initial = jnp.zeros((wanted.shape[0], width), jnp.bfloat16)
-    piece = lax.all_gather(spectra, "slab", axis=0, tiled=True)
+    piece = jnp.concatenate(
+        jax.lax.all_to_all(
+            jnp.stack([spectra] * jax.lax.axis_size("slab")),
+            concat_axis=0,
+            split_axis=0,
+            axis_name="slab",
+        ),
+        axis=0,
+    )
     inside = (wanted >= 0) & (wanted < piece.shape[0])
     chosen = jnp.take(piece, jnp.clip(wanted, 0, piece.shape[0] - 1), axis=0)
     picked = jnp.where(inside[:, None], chosen, initial)

time: 270 us -> 338 us (1.25)
  the two profiles are of different devices: /device:TPU:32 before, /device:TPU:8 now
where the time goes in v1:
time: 338 us
  waiting for transfers between devices  218 us (64%)
  other arithmetic  49.6 us (15%)
  starting transfers between devices  36.4 us (11%)
  local copies, waits for them, and re-layouts  29.4 us (9%)
  matrix products  4.41 us (1%)
    all_to_all x1, waiting for transfers between devices, local(): jax.lax.all_to_all(jnp.stack([spectra] * jax.lax.axis_size('slab')), conc...  123 us
    all_to_all x1, waiting for transfers between devices, local(): lax.all_to_all(served.reshape(regions, capacity, width), 'region', split_...  88.8 us
    another operation x3, other arithmetic  35 us
    all_to_all x1, starting transfers between devices, local(): lax.all_to_all(requests, 'region', split_axis=0, concat_axis=0, tiled=True)  13.4 us
    gather x1, local copies, waits for them, and re-layouts, local(): chosen = jnp.take(piece, jnp.clip(wanted, 0, piece.shape[0] - 1), axis=0)  12 us
    all_to_all x1, starting transfers between devices, local(): lax.all_to_all(records, 'slab', split_axis=0, concat_axis=1, tiled=True)  9.35 us
    all_to_all x1, starting transfers between devices, local(): jax.lax.all_to_all(jnp.stack([spectra] * jax.lax.axis_size('slab')), conc...  7.57 us
  transfers between devices with their start and end apart: 4, of which 3 were waited for; matrix products, arithmetic and copies ran while one was open for 15% of the time, Pallas kernels for 0%

profile of v1, /device:TPU:8, one launch (start us, length us, event | category | flops | bytes accessed | tf_op | source)
XLA Modules:
  0.0 337.5 jit_solution(3331669043079729801)
XLA Ops:
  0.0 9.4 %all-to-all-start.1 = ((bf16[32,32,128]{2,1,0:T(8,128)(2,1)}), bf16[32,32,128]{2,1,0:T(8,128)(2,1)S(1)}, u32[]{:S(2)}, u32[]{:S(2)}) async-start(bf16[32,32,128]{2,1,0:T(8,128)(2,1)} %bitcast.20), calls=%async_computation.1 | async-start | bytes 524288 | tf_op jit(solution)/shard_map/all_to_all | solution.py:58
  9.4 0.0 copy-start.2
  9.4 34.9 %negate_convert_fusion = (bf16[2048,1024]{1,0:T(8,128)(2,1)}, bf16[2048,1024]{1,0:T(8,128)(2,1)}) fusion(), kind=kLoop, calls=%fused_computation.13 | loop fusion | flops 35651584 | bytes 8388608 | tf_op jit(solution)/shard_map/convert.6
  44.3 0.0 copy-done.2
  44.3 0.1 fusion.28
  44.4 0.2 reduce_window_sum.11
  44.6 0.2 select_reduce_fusion
  44.8 1.1 scatter_custom_fusion
  45.9 0.7 all_to_all.22
  46.6 0.1 multiply_subtract_fusion
  46.6 0.0 all-to-all-done.1
  46.6 13.4 %all-to-all-start = ((s32[16,1,16]{2,1,0:T(1,128)}), s32[16,1,16]{2,1,0:T(1,128)S(1)}, u32[]{:S(2)}, u32[]{:S(2)}) async-start(s32[16,1,16]{2,1,0:T(1,128)} %all_to_all.22), calls=%async_computation | async-start | bytes 16384 | tf_op jit(solution)/shard_map/all_to_all | solution.py:71
  60.0 0.1 convert_bitcast_fusion
  60.1 0.3 copy.7
  60.4 0.1 reshape.151
  60.5 0.2 convert_reduce_fusion
  60.7 0.1 copy.8
  60.8 0.1 reduce_sum.60
  60.9 0.1 reduce_sum.61
  61.0 4.4 %fusion.3 = f32[64,2048]{1,0:T(8,128)S(1)} fusion(bf16[2048,1024]{1,0:T(8,128)(2,1)} %get-tuple-element.13, bf16[2048,1024]{1,0:T(8,128)(2,1)} %get-tuple-element.14, f32[64,2048]{1,0:T(8,128)S(1)} %reshape.151, f32[2048]{0:T(1024)S(1)} %multiply_subtract_fusion, f32[64]{0:T(128)S(1)} %broadcast_multiply_fusion.1), kind=kOutput, calls=%fused_computation.9 | convolution fusion | flops 554041344 | bytes 9445632 | tf_op jit(solution)/shard_map/dot_general | solution.py:27
  65.4 0.2 fusion.33
  65.6 0.6 fusion.22
  66.2 0.1 fusion.11
  66.3 0.1 stack_reshape.2
  66.4 6.0 %all-to-all-done = s32[16,1,16]{2,1,0:T(1,128)S(1)} async-done(((s32[16,1,16]{2,1,0:T(1,128)}), s32[16,1,16]{2,1,0:T(1,128)S(1)}, u32[]{:S(2)}, u32[]{:S(2)}) %all-to-all-start) | async-done | bytes 1056 | tf_op jit(solution)/shard_map/all_to_all | solution.py:71
  72.4 4.3 %stack.3 = bf16[32,32,4096]{2,1,0:T(8,128)(2,1)} broadcast(bf16[32,4096]{1,0:T(8,128)(2,1)S(1)} %stack_reshape.2), dimensions={1,2} | broadcast | bytes 8650752 | tf_op jit(solution)/shard_map/stack | solution.py:76
  76.7 0.0 copy-start.3
  76.7 7.6 %all-to-all-start.2 = ((bf16[32,32,4096]{2,1,0:T(8,128)(2,1)}), bf16[32,32,4096]{2,1,0:T(8,128)(2,1)}, u32[]{:S(2)}, u32[]{:S(2)}) async-start(bf16[32,32,4096]{2,1,0:T(8,128)(2,1)} %stack.3), calls=%async_computation.2 | async-start | bytes 16777216 | tf_op jit(solution)/shard_map/all_to_all | solution.py:75
  84.2 0.0 copy-done.3
  84.3 0.1 concatenate.43
  84.4 0.5 broadcast.143
  84.9 0.7 reduce.12
  85.5 0.1 concatenate.38
  85.7 122.8 %all-to-all-done.2 = bf16[32,32,4096]{2,1,0:T(8,128)(2,1)} async-done(((bf16[32,32,4096]{2,1,0:T(8,128)(2,1)}), bf16[32,32,4096]{2,1,0:T(8,128)(2,1)}, u32[]{:S(2)}, u32[]{:S(2)}) %all-to-all-start.2) | async-done | bytes 8388640 | tf_op jit(solution)/shard_map/all_to_all | solution.py:75
  208.5 12.0 %gather_fusion = bf16[384,4096]{1,0:T(8,128)(2,1)S(1)} fusion(bf16[1024,4096]{1,0:T(8,128)(2,1)} %bitcast.6, s32[1024]{0:T(1024)S(1)} %pad_clamp_fusion.1), kind=kCustom, calls=%fused_computation | custom fusion | bytes 6292992 | tf_op jit(solution)/shard_map/jit(_take)/gather | solution.py:84
  220.5 0.5 select_select_fusion
  220.9 0.0 copy-start
  221.0 1.7 copy-done
  222.6 1.5 slice.77
  224.1 6.0 %all-to-all-start.3 = ((bf16[16,16,4096]{2,1,0:T(8,128)(2,1)}), bf16[16,16,4096]{2,1,0:T(8,128)(2,1)S(1)}, u32[]{:S(2)}, u32[]{:S(2)}) async-start(bf16[16,16,4096]{2,1,0:T(8,128)(2,1)} %bitcast.19), calls=%async_computation.3 | async-start | bytes 4194304 | tf_op jit(solution)/shard_map/all_to_all | solution.py:88
  230.2 2.8 slice_convert_fusion
  233.0 4.0 %reshape.153 = f32[128,2,2,1024]{3,2,1,0:T(2,128)} reshape(f32[128,4096]{1,0:T(8,128)} %slice_convert_fusion) | data formatting | bytes 4194304 | tf_op jit(solution)/shard_map/reshape | solution.py:43
  237.0 88.8 %all-to-all-done.3 = bf16[16,16,4096]{2,1,0:T(8,128)(2,1)S(1)} async-done(((bf16[16,16,4096]{2,1,0:T(8,128)(2,1)}), bf16[16,16,4096]{2,1,0:T(8,128)(2,1)S(1)}, u32[]{:S(2)}, u32[]{:S(2)}) %all-to-all-start.3) | async-done | bytes 2097184 | tf_op jit(solution)/shard_map/all_to_all | solution.py:88
  325.8 1.2 gather_fusion.1
  327.0 0.0 copy-start.1
  327.0 1.6 gather.12
  328.6 2.2 fusion.10
  330.8 0.0 copy-done.1
  330.9 5.8 %add_reduce_fusion = (f32[128,1024]{1,0:T(8,128)S(1)}, f32[128,1024]{1,0:T(8,128)S(1)}) fusion(f32[128,2,2,1024]{3,2,1,0:T(2,128)S(1)} %fusion.10, f32[128,2,2,1024]{3,2,1,0:T(2,128)S(1)} %copy-done.1), kind=kLoop, calls=%fused_computation.23 | loop fusion | flops 1835008 | bytes 5242880 | tf_op jit(solution)/shard_map/reduce_sum | solution.py:45
  336.7 0.8 pad_maximum_fusion
  (12 shorter events, 0.2 us)
Async XLA Ops:
  0.0 46.6 %all-to-all-start.1 = ((bf16[32,32,128]{2,1,0:T(8,128)(2,1)}), bf16[32,32,128]{2,1,0:T(8,128)(2,1)S(1)}, u32[]{:S(2)}, u32[]{:S(2)}) async-start(bf16[32,32,128]{2,1,0:T(8,128)(2,1)} %bitcast.20), calls=%async_computation.1 | async-start | bytes 524288 | tf_op jit(solution)/shard_map/all_to_all | solution.py:58
  9.4 35.0 %copy-start.2 = (s32[128,1]{0,1:T(1,128)S(1)}, s32[128,1]{0,1:T(1,128)}, u32[]{:S(2)}) copy-start(s32[128,1]{0,1:T(1,128)} %param.6) | copy-start | bytes 1540
  46.6 25.8 %all-to-all-start = ((s32[16,1,16]{2,1,0:T(1,128)}), s32[16,1,16]{2,1,0:T(1,128)S(1)}, u32[]{:S(2)}, u32[]{:S(2)}) async-start(s32[16,1,16]{2,1,0:T(1,128)} %all_to_all.22), calls=%async_computation | async-start | bytes 16384 | tf_op jit(solution)/shard_map/all_to_all | solution.py:71
  76.7 7.6 %copy-start.3 = (s32[128]{0:T(128)S(1)}, s32[128]{0:T(128)}, u32[]{:S(2)}) copy-start(s32[128]{0:T(128)} %param.5) | copy-start | bytes 1540
  76.7 131.8 %all-to-all-start.2 = ((bf16[32,32,4096]{2,1,0:T(8,128)(2,1)}), bf16[32,32,4096]{2,1,0:T(8,128)(2,1)}, u32[]{:S(2)}, u32[]{:S(2)}) async-start(bf16[32,32,4096]{2,1,0:T(8,128)(2,1)} %stack.3), calls=%async_computation.2 | async-start | bytes 16777216 | tf_op jit(solution)/shard_map/all_to_all | solution.py:75
  220.9 1.7 copy-start
  224.1 101.7 %all-to-all-start.3 = ((bf16[16,16,4096]{2,1,0:T(8,128)(2,1)}), bf16[16,16,4096]{2,1,0:T(8,128)(2,1)S(1)}, u32[]{:S(2)}, u32[]{:S(2)}) async-start(bf16[16,16,4096]{2,1,0:T(8,128)(2,1)} %bitcast.19), calls=%async_computation.3 | async-start | bytes 4194304 | tf_op jit(solution)/shard_map/all_to_all | solution.py:88
  327.0 3.8 %copy-start.1 = (f32[128,2,2,1024]{3,2,1,0:T(2,128)S(1)}, f32[128,2,2,1024]{3,2,1,0:T(2,128)}, u32[]{:S(2)}) copy-start(f32[128,2,2,1024]{3,2,1,0:T(2,128)} %reshape.153) | copy-start | bytes 6291460
